TPU v7x, 32 devices: a whole 2x2x4 slice. The times are simulated.
32 devices in a mesh: ray: 4 (over x, core), vox: 8 (over z, y).
Axes of the slice: x: 2, y: 2, z: 4, core: 2. Of those that a mesh axis runs over, the one named last changes fastest.
Arguments:
- tiles: float32 [2048, 128, 128], P(('ray', 'vox')), may hold values from -0.25 to 0.25
- tile_ray: int32 [2048], P(('ray', 'vox')), may hold values from 0 to 15
- tile_vox: int32 [2048], P(('ray', 'vox')), may hold values from 0 to 511, as said below
- tile_count: int32 [32], P(('ray', 'vox')), may hold values from 1 to 64, as said below
- travel: float32 [512, 128], P(('ray', 'vox')), may hold values from -6 to 6
Outputs:
- solution: float32 [512, 128], P('vox')
- direction: float32 [512, 128], P('vox')
Inputs may be any that keep to these rules, and one draw needn't show every extreme that they name: `tile_count`: each entry is 1 to 64; some device has exactly 64 live slots. Among the 64 slots of one device (live or not), at most 16 have voxel blocks in the same range of 64 blocks (same tile_vox // 64); on every device some range is named by exactly 16 slots.
All inputs are finite; a program needn't handle non-finite values.
Results may differ from a plain program's by a relative error of at most 0.00017.
Values sent between devices are 32-bit elements; how exact they have to be, the bound alone decides.
No kernel may reach another device: no remote copies, remote signals or barrier semaphores. Data moves between devices by JAX's collectives and lax.ppermute only.
A program may use at most 64 MiB of HBM per device.

v0:
```python
import jax
import jax.numpy as jnp
from jax import lax
from jax.sharding import PartitionSpec as P

VBD = 64
ITERS = 2
HIGH = lax.Precision.HIGHEST


def on_device(tiles, tile_ray, tile_vox, tile_count, travel):
    n_vox = lax.axis_size("vox")
    blocks_all = VBD * n_vox
    tile_num = tiles.shape[0]
    ray_blocks = travel.shape[0]
    width = travel.shape[1]
    live = (jnp.arange(tile_num, dtype=jnp.int32) < tile_count[0]).astype(jnp.float32)[:, None]
    selector = (tile_ray[None, :] == jnp.arange(ray_blocks, dtype=jnp.int32)[:, None]).astype(
        jnp.float32
    )

    def backward(ray_vec):
        rows_in = jnp.dot(selector.T, ray_vec, precision=HIGH)
        prod = jnp.einsum("tij,ti->tj", tiles, rows_in, precision=HIGH) * live
        partial_sum = jnp.zeros((blocks_all, width), jnp.float32).at[tile_vox].add(prod)
        owned = lax.psum_scatter(partial_sum, "vox", scatter_dimension=0, tiled=True)
        return lax.psum(owned, "ray")

    def ray_length(ray_vec):
        return jnp.sqrt(lax.psum(jnp.sum(ray_vec * ray_vec), ("ray", "vox")))

    def vox_length(vox_vec):
        return jnp.sqrt(lax.psum(jnp.sum(vox_vec * vox_vec), "vox"))

    beta_now = ray_length(travel)
    ray_vec = travel / beta_now
    vox_vec = backward(ray_vec)
    alpha_now = vox_length(vox_vec)
    vox_vec = vox_vec / alpha_now
    direction = vox_vec
    solution = jnp.zeros_like(vox_vec)
    phibar = beta_now
    rhobar = alpha_now
    for step in range(ITERS):
        whole = lax.all_gather(vox_vec, "vox", axis=0, tiled=True)
        forward_prod = jnp.einsum("tij,tj->ti", tiles, whole[tile_vox], precision=HIGH) * live
        ray_vec = jnp.dot(selector, forward_prod, precision=HIGH) - alpha_now * ray_vec
        beta_now = ray_length(ray_vec)
        ray_vec = ray_vec / beta_now
        vox_vec = backward(ray_vec) - beta_now * vox_vec
        alpha_now = vox_length(vox_vec)
        vox_vec = vox_vec / alpha_now
        rho_val = jnp.sqrt(rhobar * rhobar + beta_now * beta_now)
        cosine = rhobar / rho_val
        sine_val = beta_now / rho_val
        theta_val = sine_val * alpha_now
        rhobar = -cosine * alpha_now
        phi_val = cosine * phibar
        phibar = sine_val * phibar
        solution = solution + phi_val / rho_val * direction
        direction = vox_vec - theta_val / rho_val * direction
    return (solution, direction)


def solution(mesh):
    return jax.shard_map(
        on_device,
        mesh=mesh,
        in_specs=(
            P(("ray", "vox"), None, None),
            P(("ray", "vox")),
            P(("ray", "vox")),
            P(("ray", "vox")),
            P(("ray", "vox"), None),
        ),
        out_specs=(P("vox", None), P("vox", None)),
        check_vma=False,
    )
```

profile of v0, /device:TPU:0, one launch (start us, length us, event | category | flops | bytes accessed | tf_op | source)
XLA Modules:
  0.0 524.3 jit_solution(6376675607895804721)
XLA Ops:
  7.2 1.3 multiply_reduce_fusion.5
  8.5 42.2 %psum.63 = f32[]{:T(128)} all-reduce(f32[]{:T(128)} %multiply_reduce_fusion.5), channel_id=1, replica_groups=mesh['ray'=4,'vox'=8] {'ray','vox'}, use_global_device_ids=true, to_apply=%region_1.0 | all-reduce | flops 1 | bytes 8 | tf_op jit(solution)/shard_map/psum | solution.py:30
  51.4 0.7 compare_select_fusion
  52.7 0.9 fusion.19
  53.7 5.3 %fusion.26 = f32[64,1,128]{2,1,0:T(1,128)S(1)} fusion(f32[64,128,1]{1,2,0:T(1,128)S(1)} %bitcast.43, f32[64,128,128]{2,1,0:T(8,128)} %param.5), kind=kOutput, calls=%fused_computation.52 | convolution fusion | flops 12582912 | bytes 4259840 | tf_op jit(solution)/shard_map/tij,ti->tj/dot_general | solution.py:24
  59.0 1.5 scatter_custom_fusion
  60.6 61.7 %reduce-scatter.4.cloned.1.call-done = f32[64,128]{1,0:T(8,128)} async-done(((f32[512,128]{1,0:T(8,128)}), f32[64,128]{1,0:T(8,128)}) %reduce-scatter.4.cloned.1.call-update) | async-done | bytes 32784 | tf_op jit(solution)/shard_map/reduce_scatter | solution.py:26
  122.3 10.8 %psum.64 = f32[64,128]{1,0:T(8,128)S(1)} all-reduce(f32[64,128]{1,0:T(8,128)} %reduce-scatter.4.cloned.1.call-done), channel_id=1, replica_groups=mesh['ray'=4,'vox'=8] {'ray'}, use_global_device_ids=true, to_apply=%region_4.0 | all-reduce | flops 8192 | bytes 65536 | tf_op jit(solution)/shard_map/psum | solution.py:27
  133.1 0.6 multiply_reduce_fusion.2
  133.7 20.1 %psum.65 = f32[]{:T(128)} all-reduce(f32[]{:T(128)} %multiply_reduce_fusion.2), channel_id=1, replica_groups=mesh['ray'=4,'vox'=8] {'vox'}, use_global_device_ids=true, to_apply=%region_6.0 | all-reduce | flops 1 | bytes 8 | tf_op jit(solution)/shard_map/psum | solution.py:33
  154.5 30.9 %all_gather.6 = f32[512,128]{1,0:T(8,128)S(1)} all-gather(f32[64,128]{1,0:T(8,128)S(1)} %broadcast_divide_fusion.1), channel_id=1, replica_groups=mesh['ray'=4,'vox'=8] {'vox'}, dimensions={0}, use_global_device_ids=true | all-gather | bytes 294912 | tf_op jit(solution)/shard_map/all_gather | solution.py:45
  185.4 0.6 gather_fusion
  186.0 8.3 %fusion.27 = f32[64,1,128]{2,1,0:T(1,128)S(1)} fusion(f32[64,128,1]{1,2,0:T(1,128)S(1)} %bitcast.40, f32[64,128,128]{2,1,0:T(8,128)} %param.5), kind=kOutput, calls=%fused_computation.53 | convolution fusion | flops 12582912 | bytes 4259840 | tf_op jit(solution)/shard_map/tij,tj->ti/dot_general | solution.py:46
  194.3 0.8 multiply_reduce_fusion.4
  195.2 37.1 %psum.66 = f32[]{:T(128)} all-reduce(f32[]{:T(128)} %get-tuple-element.4), channel_id=1, replica_groups=mesh['ray'=4,'vox'=8] {'ray','vox'}, use_global_device_ids=true, to_apply=%region_8.0 | all-reduce | flops 1 | bytes 8 | tf_op jit(solution)/shard_map/psum | solution.py:30
  233.2 5.3 %fusion.28 = f32[64,1,128]{2,1,0:T(1,128)S(1)} fusion(f32[64,128,1]{1,2,0:T(1,128)S(1)} %bitcast.44, f32[64,128,128]{2,1,0:T(8,128)} %param.5), kind=kOutput, calls=%fused_computation.54 | convolution fusion | flops 12582912 | bytes 4259840 | tf_op jit(solution)/shard_map/tij,ti->tj/dot_general | solution.py:24
  238.5 1.5 scatter_custom_fusion.1
  240.1 63.4 %reduce-scatter.6.cloned.1.call-done = f32[64,128]{1,0:T(8,128)} async-done(((f32[512,128]{1,0:T(8,128)}), f32[64,128]{1,0:T(8,128)}) %reduce-scatter.6.cloned.1.call-update) | async-done | bytes 32784 | tf_op jit(solution)/shard_map/reduce_scatter | solution.py:26
  303.4 10.8 %psum.67 = f32[64,128]{1,0:T(8,128)S(1)} all-reduce(f32[64,128]{1,0:T(8,128)} %reduce-scatter.6.cloned.1.call-done), channel_id=1, replica_groups=mesh['ray'=4,'vox'=8] {'ray'}, use_global_device_ids=true, to_apply=%region_11.0 | all-reduce | flops 8192 | bytes 65536 | tf_op jit(solution)/shard_map/psum | solution.py:27
  314.2 0.6 multiply_reduce_fusion.1
  314.9 20.1 %psum.68 = f32[]{:T(128)} all-reduce(f32[]{:T(128)} %multiply_reduce_fusion.1), channel_id=1, replica_groups=mesh['ray'=4,'vox'=8] {'vox'}, use_global_device_ids=true, to_apply=%region_13.0 | all-reduce | flops 1 | bytes 8 | tf_op jit(solution)/shard_map/psum | solution.py:33
  335.7 31.1 %all_gather.7 = f32[512,128]{1,0:T(8,128)S(1)} all-gather(f32[64,128]{1,0:T(8,128)S(1)} %broadcast_divide_fusion), channel_id=1, replica_groups=mesh['ray'=4,'vox'=8] {'vox'}, dimensions={0}, use_global_device_ids=true | all-gather | bytes 294912 | tf_op jit(solution)/shard_map/all_gather | solution.py:45
  367.3 8.3 %fusion.29 = f32[64,1,128]{2,1,0:T(1,128)S(1)} fusion(f32[64,128,1]{1,2,0:T(1,128)S(1)} %bitcast.38, f32[64,128,128]{2,1,0:T(8,128)} %param.5), kind=kOutput, calls=%fused_computation.55 | convolution fusion | flops 12582912 | bytes 4259840 | tf_op jit(solution)/shard_map/tij,tj->ti/dot_general | solution.py:46
  375.6 0.8 multiply_reduce_fusion.3
  376.4 37.1 %psum.69 = f32[]{:T(128)} all-reduce(f32[]{:T(128)} %get-tuple-element.6), channel_id=1, replica_groups=mesh['ray'=4,'vox'=8] {'ray','vox'}, use_global_device_ids=true, to_apply=%region_15.0 | all-reduce | flops 1 | bytes 8 | tf_op jit(solution)/shard_map/psum | solution.py:30
  414.5 5.3 %fusion.30 = f32[64,1,128]{2,1,0:T(1,128)S(1)} fusion(f32[64,128,1]{1,2,0:T(1,128)S(1)} %bitcast.42, f32[64,128,128]{2,1,0:T(8,128)} %param.5), kind=kOutput, calls=%fused_computation.56 | convolution fusion | flops 12582912 | bytes 4259840 | tf_op jit(solution)/shard_map/tij,ti->tj/dot_general | solution.py:24
  419.8 1.5 scatter_custom_fusion.2
  421.7 63.1 %reduce-scatter.8.cloned.1.call-done = f32[64,128]{1,0:T(8,128)} async-done(((f32[512,128]{1,0:T(8,128)}), f32[64,128]{1,0:T(8,128)}) %reduce-scatter.8.cloned.1.call-update) | async-done | bytes 32784 | tf_op jit(solution)/shard_map/reduce_scatter | solution.py:26
  484.8 10.8 %psum.70 = f32[64,128]{1,0:T(8,128)S(1)} all-reduce(f32[64,128]{1,0:T(8,128)} %reduce-scatter.8.cloned.1.call-done), channel_id=1, replica_groups=mesh['ray'=4,'vox'=8] {'ray'}, use_global_device_ids=true, to_apply=%region_18.0 | all-reduce | flops 8192 | bytes 65536 | tf_op jit(solution)/shard_map/psum | solution.py:27
  495.6 0.6 multiply_reduce_fusion
  496.2 20.1 %psum.71 = f32[]{:T(128)} all-reduce(f32[]{:T(128)} %multiply_reduce_fusion), channel_id=1, replica_groups=mesh['ray'=4,'vox'=8] {'vox'}, use_global_device_ids=true, to_apply=%region_20.0 | all-reduce | flops 1 | bytes 8 | tf_op jit(solution)/shard_map/psum | solution.py:33
  517.1 0.7 multiply_subtract_fusion
  (17 shorter events, 1.2 us)
Async XLA Ops:
  7.2 115.2 %reduce-scatter.4.cloned.1.call-start = ((), (), s32[]{:S(2)}) async-start(), calls=%async_computation.3 | async-start | bytes 294912 | tf_op jit(solution)/shard_map/reduce_scatter | solution.py:26
  53.7 140.7 %copy-start = (f32[16,128]{1,0:T(8,128)S(1)}, f32[16,128]{1,0:T(8,128)}, u32[]{:S(2)}) copy-start(f32[16,128]{1,0:T(8,128)} %param.9) | copy-start | bytes 24580
  53.7 140.7 %copy-start.1 = (s32[64]{0:T(128)S(1)}, s32[64]{0:T(128)}, u32[]{:S(2)}) copy-start(s32[64]{0:T(128)} %param.6) | copy-start | bytes 772
  60.5 242.9 %reduce-scatter.6.cloned.1.call-start = ((), (), s32[]{:S(2)}) async-start(), calls=%async_computation.4 | async-start | bytes 294912 | tf_op jit(solution)/shard_map/reduce_scatter | solution.py:26
  240.0 244.7 %reduce-scatter.8.cloned.1.call-start = ((), (), s32[]{:S(2)}) async-start(), calls=%async_computation.5 | async-start | bytes 294912 | tf_op jit(solution)/shard_map/reduce_scatter | solution.py:26
Sparse Core Ops, SparseCore 0:
  60.7 61.6 reduce-scatter.3
  240.2 63.2 reduce-scatter.5
  421.5 63.2 reduce-scatter.7
where the time goes:
time: 526 us; the launch traced here: 524 us
  blocking collectives  271 us (52%)
  waiting for transfers between devices  188 us (36%)
  matrix products  35.5 us (7%)
  between operations  19.1 us (4%)
  other arithmetic  9.11 us (2%)
    reduce_scatter x3, waiting for transfers between devices, backward(): lax.psum_scatter(partial_sum, 'vox', scatter_dimension=0, tiled=True)  188 us
    psum x3, blocking collectives, ray_length(): return jnp.sqrt(lax.psum(jnp.sum(ray_vec * ray_vec), ('ray', 'vox')))  116 us
    all_gather x2, blocking collectives, on_device(): whole = lax.all_gather(vox_vec, 'vox', axis=0, tiled=True)  62 us
    psum x3, blocking collectives, vox_length(): return jnp.sqrt(lax.psum(jnp.sum(vox_vec * vox_vec), 'vox'))  60.2 us
    psum x3, blocking collectives, backward(): return lax.psum(owned, 'ray')  32.4 us
    dot_general x2, matrix products, on_device(): jnp.einsum('tij,tj->ti', tiles, whole[tile_vox], precision=HIGH) * live  16.6 us
    dot_general x3, matrix products, backward(): prod = jnp.einsum('tij,ti->tj', tiles, rows_in, precision=HIGH) * live  15.8 us
  transfers between devices with their start and end apart: 3, of which 3 were waited for; matrix products, arithmetic and copies ran while one was open for 0% of the time, Pallas kernels for 0%

commit v1 on v0

--- a/solution.py
+++ b/solution.py
@@ -24,7 +24,7 @@
         prod = jnp.einsum("tij,ti->tj", tiles, rows_in, precision=HIGH) * live
         partial_sum = jnp.zeros((blocks_all, width), jnp.float32).at[tile_vox].add(prod)
         owned = lax.psum_scatter(partial_sum, "vox", scatter_dimension=0, tiled=True)
-        return lax.psum(owned, "ray")
+        return jnp.sum(lax.all_gather(owned, "ray"), axis=0)
 
     def ray_length(ray_vec):
         return jnp.sqrt(lax.psum(jnp.sum(ray_vec * ray_vec), ("ray", "vox")))

time: 526 us -> 509 us (0.968)
  blocking collectives: 271 us -> 255 us
    psum x3 -> x0, blocking collectives: 32.4 us -> none  [backward(): return lax.psum(owned, 'ray')]
    all_gather x0 -> x3, blocking collectives: none -> 16.9 us  [backward(): return jnp.sum(lax.all_gather(owned, 'ray'), axis=0)]
where the time goes in v1:
time: 509 us; the launch traced here: 508 us
  blocking collectives  255 us (50%)
  waiting for transfers between devices  188 us (37%)
  matrix products  35.5 us (7%)
  between operations  19.1 us (4%)
  other arithmetic  9.14 us (2%)
    reduce_scatter x3, waiting for transfers between devices, backward(): lax.psum_scatter(partial_sum, 'vox', scatter_dimension=0, tiled=True)  188 us
    psum x3, blocking collectives, ray_length(): return jnp.sqrt(lax.psum(jnp.sum(ray_vec * ray_vec), ('ray', 'vox')))  116 us
    all_gather x2, blocking collectives, on_device(): whole = lax.all_gather(vox_vec, 'vox', axis=0, tiled=True)  61.7 us
    psum x3, blocking collectives, vox_length(): return jnp.sqrt(lax.psum(jnp.sum(vox_vec * vox_vec), 'vox'))  60.2 us
    all_gather x3, blocking collectives, backward(): return jnp.sum(lax.all_gather(owned, 'ray'), axis=0)  16.9 us
    dot_general x2, matrix products, on_device(): jnp.einsum('tij,tj->ti', tiles, whole[tile_vox], precision=HIGH) * live  16.6 us
    dot_general x3, matrix products, backward(): prod = jnp.einsum('tij,ti->tj', tiles, rows_in, precision=HIGH) * live  15.8 us
  transfers between devices with their start and end apart: 3, of which 3 were waited for; matrix products, arithmetic and copies ran while one was open for 0% of the time, Pallas kernels for 0%

profile of v1, /device:TPU:0, one launch (start us, length us, event | category | flops | bytes accessed | tf_op | source)
XLA Modules:
  0.0 508.2 jit_solution(10229904004232865640)
XLA Ops:
  7.2 1.3 multiply_reduce_fusion.5
  8.5 42.2 %psum.42 = f32[]{:T(128)} all-reduce(f32[]{:T(128)} %multiply_reduce_fusion.5), channel_id=1, replica_groups=mesh['ray'=4,'vox'=8] {'ray','vox'}, use_global_device_ids=true, to_apply=%region_1.0 | all-reduce | flops 1 | bytes 8 | tf_op jit(solution)/shard_map/psum | solution.py:30
  51.4 0.7 compare_select_fusion
  52.7 0.9 fusion.19
  53.7 5.3 %fusion.26 = f32[64,1,128]{2,1,0:T(1,128)S(1)} fusion(f32[64,128,1]{1,2,0:T(1,128)S(1)} %bitcast.49, f32[64,128,128]{2,1,0:T(8,128)} %param.5), kind=kOutput, calls=%fused_computation.52 | convolution fusion | flops 12582912 | bytes 4259840 | tf_op jit(solution)/shard_map/tij,ti->tj/dot_general | solution.py:24
  59.0 1.5 scatter_custom_fusion
  60.6 61.7 %reduce-scatter.4.cloned.1.call-done = f32[64,128]{1,0:T(8,128)} async-done(((f32[512,128]{1,0:T(8,128)}), f32[64,128]{1,0:T(8,128)}) %reduce-scatter.4.cloned.1.call-update) | async-done | bytes 32784 | tf_op jit(solution)/shard_map/reduce_scatter | solution.py:26
  122.3 5.6 %all-gather = f32[256,128]{1,0:T(8,128)S(1)} all-gather(f32[64,128]{1,0:T(8,128)} %reduce-scatter.4.cloned.1.call-done), channel_id=2, replica_groups=mesh['ray'=4,'vox'=8] {'ray'}, dimensions={0}, use_global_device_ids=true | all-gather | bytes 163840 | tf_op jit(solution)/shard_map/all_gather | solution.py:27
  128.0 0.6 multiply_reduce_fusion.2
  128.6 20.1 %psum.43 = f32[]{:T(128)} all-reduce(f32[]{:T(128)} %multiply_reduce_fusion.2), channel_id=1, replica_groups=mesh['ray'=4,'vox'=8] {'vox'}, use_global_device_ids=true, to_apply=%region_6.0 | all-reduce | flops 1 | bytes 8 | tf_op jit(solution)/shard_map/psum | solution.py:33
  149.3 30.7 %all_gather.26 = f32[512,128]{1,0:T(8,128)S(1)} all-gather(f32[64,128]{1,0:T(8,128)S(1)} %broadcast_divide_fusion.1), channel_id=1, replica_groups=mesh['ray'=4,'vox'=8] {'vox'}, dimensions={0}, use_global_device_ids=true | all-gather | bytes 294912 | tf_op jit(solution)/shard_map/all_gather | solution.py:45
  180.1 0.6 gather_fusion
  180.7 8.3 %fusion.27 = f32[64,1,128]{2,1,0:T(1,128)S(1)} fusion(f32[64,128,1]{1,2,0:T(1,128)S(1)} %bitcast.46, f32[64,128,128]{2,1,0:T(8,128)} %param.5), kind=kOutput, calls=%fused_computation.53 | convolution fusion | flops 12582912 | bytes 4259840 | tf_op jit(solution)/shard_map/tij,tj->ti/dot_general | solution.py:46
  189.0 0.8 multiply_reduce_fusion.4
  189.8 37.1 %psum.44 = f32[]{:T(128)} all-reduce(f32[]{:T(128)} %get-tuple-element.4), channel_id=1, replica_groups=mesh['ray'=4,'vox'=8] {'ray','vox'}, use_global_device_ids=true, to_apply=%region_8.0 | all-reduce | flops 1 | bytes 8 | tf_op jit(solution)/shard_map/psum | solution.py:30
  227.8 5.3 %fusion.28 = f32[64,1,128]{2,1,0:T(1,128)S(1)} fusion(f32[64,128,1]{1,2,0:T(1,128)S(1)} %bitcast.50, f32[64,128,128]{2,1,0:T(8,128)} %param.5), kind=kOutput, calls=%fused_computation.54 | convolution fusion | flops 12582912 | bytes 4259840 | tf_op jit(solution)/shard_map/tij,ti->tj/dot_general | solution.py:24
  233.1 1.5 scatter_custom_fusion.1
  234.7 63.3 %reduce-scatter.6.cloned.1.call-done = f32[64,128]{1,0:T(8,128)} async-done(((f32[512,128]{1,0:T(8,128)}), f32[64,128]{1,0:T(8,128)}) %reduce-scatter.6.cloned.1.call-update) | async-done | bytes 32784 | tf_op jit(solution)/shard_map/reduce_scatter | solution.py:26
  298.0 5.6 %all-gather.1 = f32[256,128]{1,0:T(8,128)S(1)} all-gather(f32[64,128]{1,0:T(8,128)} %reduce-scatter.6.cloned.1.call-done), channel_id=3, replica_groups=mesh['ray'=4,'vox'=8] {'ray'}, dimensions={0}, use_global_device_ids=true | all-gather | bytes 163840 | tf_op jit(solution)/shard_map/all_gather | solution.py:27
  303.6 0.6 multiply_reduce_fusion.1
  304.3 20.0 %psum.45 = f32[]{:T(128)} all-reduce(f32[]{:T(128)} %multiply_reduce_fusion.1), channel_id=1, replica_groups=mesh['ray'=4,'vox'=8] {'vox'}, use_global_device_ids=true, to_apply=%region_13.0 | all-reduce | flops 1 | bytes 8 | tf_op jit(solution)/shard_map/psum | solution.py:33
  325.0 30.9 %all_gather.29 = f32[512,128]{1,0:T(8,128)S(1)} all-gather(f32[64,128]{1,0:T(8,128)S(1)} %broadcast_divide_fusion), channel_id=1, replica_groups=mesh['ray'=4,'vox'=8] {'vox'}, dimensions={0}, use_global_device_ids=true | all-gather | bytes 294912 | tf_op jit(solution)/shard_map/all_gather | solution.py:45
  356.5 8.3 %fusion.29 = f32[64,1,128]{2,1,0:T(1,128)S(1)} fusion(f32[64,128,1]{1,2,0:T(1,128)S(1)} %bitcast.44, f32[64,128,128]{2,1,0:T(8,128)} %param.5), kind=kOutput, calls=%fused_computation.55 | convolution fusion | flops 12582912 | bytes 4259840 | tf_op jit(solution)/shard_map/tij,tj->ti/dot_general | solution.py:46
  364.8 0.8 multiply_reduce_fusion.3
  365.7 37.1 %psum.46 = f32[]{:T(128)} all-reduce(f32[]{:T(128)} %get-tuple-element.6), channel_id=1, replica_groups=mesh['ray'=4,'vox'=8] {'ray','vox'}, use_global_device_ids=true, to_apply=%region_15.0 | all-reduce | flops 1 | bytes 8 | tf_op jit(solution)/shard_map/psum | solution.py:30
  403.6 5.3 %fusion.30 = f32[64,1,128]{2,1,0:T(1,128)S(1)} fusion(f32[64,128,1]{1,2,0:T(1,128)S(1)} %bitcast.48, f32[64,128,128]{2,1,0:T(8,128)} %param.5), kind=kOutput, calls=%fused_computation.56 | convolution fusion | flops 12582912 | bytes 4259840 | tf_op jit(solution)/shard_map/tij,ti->tj/dot_general | solution.py:24
  408.9 1.5 scatter_custom_fusion.2
  410.9 63.0 %reduce-scatter.8.cloned.1.call-done = f32[64,128]{1,0:T(8,128)} async-done(((f32[512,128]{1,0:T(8,128)}), f32[64,128]{1,0:T(8,128)}) %reduce-scatter.8.cloned.1.call-update) | async-done | bytes 32784 | tf_op jit(solution)/shard_map/reduce_scatter | solution.py:26
  473.9 5.6 %all-gather.2 = f32[256,128]{1,0:T(8,128)S(1)} all-gather(f32[64,128]{1,0:T(8,128)} %reduce-scatter.8.cloned.1.call-done), channel_id=4, replica_groups=mesh['ray'=4,'vox'=8] {'ray'}, dimensions={0}, use_global_device_ids=true | all-gather | bytes 163840 | tf_op jit(solution)/shard_map/all_gather | solution.py:27
  479.5 0.6 multiply_reduce_fusion
  480.1 20.1 %psum.47 = f32[]{:T(128)} all-reduce(f32[]{:T(128)} %multiply_reduce_fusion), channel_id=1, replica_groups=mesh['ray'=4,'vox'=8] {'vox'}, use_global_device_ids=true, to_apply=%region_20.0 | all-reduce | flops 1 | bytes 8 | tf_op jit(solution)/shard_map/psum | solution.py:33
  501.0 0.7 multiply_subtract_fusion
  (20 shorter events, 1.3 us)
Async XLA Ops:
  7.2 115.2 %reduce-scatter.4.cloned.1.call-start = ((), (), s32[]{:S(2)}) async-start(), calls=%async_computation.3 | async-start | bytes 294912 | tf_op jit(solution)/shard_map/reduce_scatter | solution.py:26
  53.7 135.3 %copy-start = (f32[16,128]{1,0:T(8,128)S(1)}, f32[16,128]{1,0:T(8,128)}, u32[]{:S(2)}) copy-start(f32[16,128]{1,0:T(8,128)} %param.9) | copy-start | bytes 24580
  53.7 135.3 %copy-start.1 = (s32[64]{0:T(128)S(1)}, s32[64]{0:T(128)}, u32[]{:S(2)}) copy-start(s32[64]{0:T(128)} %param.6) | copy-start | bytes 772
  60.5 237.5 %reduce-scatter.6.cloned.1.call-start = ((), (), s32[]{:S(2)}) async-start(), calls=%async_computation.4 | async-start | bytes 294912 | tf_op jit(solution)/shard_map/reduce_scatter | solution.py:26
  234.7 239.2 %reduce-scatter.8.cloned.1.call-start = ((), (), s32[]{:S(2)}) async-start(), calls=%async_computation.5 | async-start | bytes 294912 | tf_op jit(solution)/shard_map/reduce_scatter | solution.py:26
Sparse Core Ops, SparseCore 0:
  60.7 61.6 reduce-scatter.3
  234.8 63.1 reduce-scatter.5
  410.6 63.1 reduce-scatter.7
